TPU v7x, 256 devices: a whole 4x4x8 slice. The times are simulated.
256 devices in a mesh: member: 8 (over y, x_hi), space: 32 (over z, x_lo, core).
Axes of the slice: x: 4 (x_hi: 2, x_lo: 2; x = x_hi * 2 + x_lo), y: 4, z: 8, core: 2. Of those that a mesh axis runs over, the one named last changes fastest.
Arguments:
- zonal_wind: bfloat16 [48, 256, 256, 128], P('member', 'space'), may hold values from -6 to 6
- meridional_wind: bfloat16 [48, 256, 256, 128], P('member', 'space'), may hold values from -6 to 6
- heat_anomaly: bfloat16 [48, 256, 256, 128], P('member', 'space'), may hold values from -6 to 6
- moisture_anomaly: bfloat16 [48, 256, 256, 128], P('member', 'space'), may hold values from -6 to 6
- projection_scale: float32 [256, 256], P('space'), may hold values from 0.5 to 2
- balance_multiplier: float32 [256, 256], P('space'), may hold values from -4 to 4
- heat_on_curl_slope: float32 [128], replicated, may hold values from 0.3 to 1.5
- moisture_on_heat_slope: float32 [128], replicated, may hold values from 0.3 to 1.5
Outputs:
- covariance: float32 [32, 512, 512], P('space', 'member')
All inputs are finite; a program needn't handle non-finite values.
Results may differ from a plain program's by a relative error of at most 0.0009.
Values may be sent and summed in bfloat16 or wider, within the bound.
No kernel may reach another device: no remote copies, remote signals or barrier semaphores. Data moves between devices by JAX's collectives and lax.ppermute only.
A program may use at most 128 MiB of HBM per device.

v0:
```python
import jax
import jax.numpy as jnp
from jax import lax
from jax.sharding import PartitionSpec as P


def extended(block, sides, width):
    for axis, dim in sides:
        count = lax.axis_size(axis)
        forward = [(i, i + 1) for i in range(count - 1)]
        backward = [(target, source) for source, target in forward]
        low = lax.ppermute(
            lax.slice_in_dim(block, block.shape[dim] - width, None, axis=dim), axis, forward
        )
        high = lax.ppermute(lax.slice_in_dim(block, 0, width, axis=dim), axis, backward)
        block = jnp.concatenate([low, block, high], axis=dim)
    return block


def lat_diff(padded):
    return (-padded[:, 4:] + 8.0 * padded[:, 3:-1] - 8.0 * padded[:, 1:-3] + padded[:, :-4]) / 12.0


def lon_diff(field):
    return (jnp.roll(field, -1, 2) - jnp.roll(field, 1, 2)) / 2.0


def gram_rows(left, right, precision):
    return lax.dot_general(
        left,
        right,
        (((0,), (0,)), ((), ())),
        preferred_element_type=jnp.float32,
        precision=precision,
    )


def on_device(
    zonal_wind,
    meridional_wind,
    heat_anomaly,
    moisture_anomaly,
    projection_scale,
    balance_multiplier,
    heat_on_curl_slope,
    moisture_on_heat_slope,
):
    winds = jnp.stack([zonal_wind, meridional_wind])
    padded = extended(winds, (("space", 2),), 2)
    u_full = padded[0].astype(jnp.float32)
    v_full = padded[1].astype(jnp.float32)
    u_mid = u_full[:, 2:-2]
    v_mid = v_full[:, 2:-2]
    factor = projection_scale[None, :, :, None]
    wind_curl = factor * (lon_diff(v_mid) - lat_diff(u_full))
    wind_spreading = factor * (lon_diff(u_mid) + lat_diff(v_full))
    heat_residual = (
        heat_anomaly.astype(jnp.float32)
        - heat_on_curl_slope * balance_multiplier[None, :, :, None] * wind_curl
    )
    moisture_residual = (
        moisture_anomaly.astype(jnp.float32) - moisture_on_heat_slope * heat_residual
    )
    sample_vector = jnp.concatenate(
        [wind_curl, wind_spreading, heat_residual, moisture_residual], axis=3
    ).astype(jnp.bfloat16)
    width = sample_vector.shape[3]
    groups = lax.axis_size("member")
    members_all = float(sample_vector.shape[0] * groups)
    rows = width // groups
    scale = 1.0 / (
        (sample_vector.shape[0] * groups - 1) * sample_vector.shape[1] * sample_vector.shape[2]
    )
    local_sum = jnp.sum(sample_vector.astype(jnp.float32), axis=0)
    highest = lax.Precision.HIGHEST
    totals = lax.psum(local_sum.astype(jnp.bfloat16), "member").astype(jnp.float32)
    ens_mean = totals / members_all
    anomaly = (sample_vector.astype(jnp.float32) - ens_mean[None]).reshape(-1, width)
    summed = lax.psum(gram_rows(anomaly, anomaly, highest), "member")
    mine = lax.dynamic_slice_in_dim(summed, lax.axis_index("member") * rows, rows, 0)
    return (mine * scale)[None]


def solution(mesh):
    placed = (
        P("member", "space", None, None),
        P("member", "space", None, None),
        P("member", "space", None, None),
        P("member", "space", None, None),
        P("space", None),
        P("space", None),
        P(),
        P(),
    )
    return jax.shard_map(
        on_device, mesh=mesh, in_specs=placed, out_specs=P("space", "member", None), check_vma=False
    )
```

profile of v0, /device:TPU:32, one launch (start us, length us, event | category | flops | bytes accessed | tf_op | source)
XLA Modules:
  0.0 398.0 jit_solution(15187263086016481652)
XLA Ops:
  6.5 0.0 all-reduce.3.cloned.1.call-start
  6.5 2.3 pad_maximum_fusion.4
  8.8 2.1 collective-permute-start
  10.9 4.5 %collective-permute-start.1 = (bf16[2,6,2,256,128]{4,3,2,1,0:T(8,128)(2,1)S(1)}, bf16[2,6,2,256,128]{4,3,2,1,0:T(8,128)(2,1)S(1)}, u32[]{:S(2)}, u32[]{:S(2)}) collective-permute-start(bf16[2,6,2,256,128]{4,3,2,1,0:T(8,128)(2,1)S(1)} %get-tuple-element.20), channel_id=1, source_target_pairs={{1,0},{2,1},{3,2},{4,3},{5,4},{6,5},{7,6},{8,7},{9,8},{10,9},{11,1... | collective-permute-start | bytes 4718600 | tf_op jit(solution)/shard_map/ppermute | solution.py:15
  15.4 0.0 copy-done.7
  15.4 0.0 copy-done.9
  15.5 1.3 broadcast_multiply_fusion
  16.8 14.9 %collective-permute-done = bf16[2,6,2,256,128]{4,3,2,1,0:T(8,128)(2,1)S(1)} collective-permute-done((bf16[2,6,2,256,128]{4,3,2,1,0:T(8,128)(2,1)S(1)}, bf16[2,6,2,256,128]{4,3,2,1,0:T(8,128)(2,1)S(1)}, u32[]{:S(2)}, u32[]{:S(2)}) %collective-permute-start) | collective-permute-done | bytes 1572896 | tf_op jit(solution)/shard_map/ppermute | solution.py:12
  31.7 1.7 collective-permute-done.1
  33.4 0.0 copy-done.4
  33.4 0.0 copy-done.5
  33.4 4.4 %pad_maximum_fusion.1 = bf16[2,6,12,256,128]{4,3,2,1,0:T(8,128)(2,1)} fusion(bf16[2,6,2,256,128]{4,3,2,1,0:T(8,128)(2,1)S(1)} %collective-permute-done.1, bf16[1,6,8,256,128]{4,3,2,1,0:T(8,128)(2,1)S(1)} %bitcast.21, bf16[1,6,8,256,128]{4,3,2,1,0:T(8,128)(2,1)S(1)} %bitcast.23, bf16[2,6,2,256,128]{4,3,2,1,0:T(8,128)(2,1)S(1)} %collective-permute-done), kind=kLoop, calls=%fused_computation.5 | loop fusion | flops 14155776 | bytes 18874368 | tf_op jit(solution)/shard_map/concatenate | solution.py:16
  37.8 12.8 %fusion.18 = (f32[6,12,256,128]{3,2,1,0:T(8,128)}, f32[6,12,256,128]{3,2,1,0:T(8,128)}) fusion(bf16[2,6,12,256,128]{4,3,2,1,0:T(8,128)(2,1)} %pad_maximum_fusion.1), kind=kLoop, calls=%fused_computation.34 | loop fusion | flops 4718592 | bytes 28311552 | tf_op jit(solution)/shard_map/convert_element_type | solution.py:51
  50.6 1.3 fusion.27
  51.9 0.0 copy-start.8
  51.9 15.6 %fusion.28 = (f32[6,8,255,128]{3,2,1,0:T(8,128)S(1)}, f32[6,8,255,128]{3,2,1,0:T(8,128)}, f32[6,8,255,128]{3,2,1,0:T(8,128)}, f32[6,8,255,128]{3,2,1,0:T(8,128)}) fusion(f32[6,12,256,128]{3,2,1,0:T(8,128)} %get-tuple-element.18, f32[6,12,256,128]{3,2,1,0:T(8,128)} %get-tuple-element.17), kind=kLoop, calls=%fused_computation.46 | loop fusion | bytes 50135040 | tf_op jit(solution)/shard_map/jit(_roll_static)/slice | solution.py:25
  67.6 0.0 copy-done.8
  67.6 27.2 %fusion.25 = (bf16[6,8,256,128]{3,2,1,0:T(8,128)(2,1)S(1)}, f32[6,8,256,128]{3,2,1,0:T(8,128)}, bf16[6,8,256,128]{3,2,1,0:T(8,128)(2,1)}) fusion(f32[6,12,256,128]{3,2,1,0:T(8,128)} %get-tuple-element.18, f32[6,8,255,128]{3,2,1,0:T(8,128)} %get-tuple-element.24, f32[6,8,1,128]{3,2,1,0:T(1,128)S(1)} %get-tuple-element.22, ...), kind=kLoop, calls=%fused_computation.44 | loop fusion | flops 44040192 | bytes 88088576 | tf_op jit(solution)/shard_map/convert.3
  94.8 9.8 %fusion.19 = (bf16[6,8,256,128]{3,2,1,0:T(8,128)(2,1)S(1)}, bf16[6,8,256,128]{3,2,1,0:T(8,128)(2,1)}) fusion(f32[6,8,256,128]{3,2,1,0:T(8,128)} %get-tuple-element.6, bf16[6,8,256,128]{3,2,1,0:T(8,128)(2,1)} %param.10, f32[8,256,128]{2,1,0:T(8,128)} %broadcast_multiply_fusion, f32[128]{0:T(128)S(1)} %copy-done.10, bf16[6,8,256,128]{3,2,1,0:T(8,128)(2,1)} %param.11), kind=kLoop, calls=%fused_computation.36 | loop fusion | flops 12582912 | bytes 19923456 | tf_op jit(solution)/shard_map/convert.5
  104.6 0.0 copy-done
  104.6 1.7 copy-done.6
  106.3 0.0 copy-done.2
  106.3 8.1 %fusion.20 = bf16[8,256,512]{2,1,0:T(8,128)(2,1)} fusion(bf16[6,8,256,128]{3,2,1,0:T(8,128)(2,1)} %get-tuple-element.8, bf16[6,8,256,128]{3,2,1,0:T(8,128)(2,1)S(1)} %get-tuple-element.7, bf16[6,8,256,128]{3,2,1,0:T(8,128)(2,1)S(1)} %copy-done.2, bf16[6,8,256,128]{3,2,1,0:T(8,128)(2,1)S(1)} %get-tuple-element.5), kind=kLoop, calls=%fused_computation.37 | loop fusion | flops 55574528 | bytes 14680064 | tf_op jit(solution)/shard_map/reduce_sum | solution.py:74
  114.4 0.0 all-reduce.3.cloned.1.call-update
  114.4 0.2 all-reduce.5.cloned.1.call-start
  114.6 130.1 %all-reduce.3.cloned.1.call-done = bf16[8,256,512]{2,1,0:T(8,128)(2,1)} async-done(((bf16[8,256,512]{2,1,0:T(8,128)(2,1)}), bf16[8,256,512]{2,1,0:T(8,128)(2,1)}) %all-reduce.3.cloned.1.call-update) | async-done | bytes 2097168 | tf_op jit(solution)/shard_map/psum | solution.py:76
  244.7 2.4 convert_multiply_fusion
  247.1 0.1 copy-done.3
  247.2 47.7 %fusion.21 = f32[512,512]{1,0:T(8,128)} fusion(f32[8,256,512]{2,1,0:T(8,128)S(1)} %convert_multiply_fusion, bf16[6,8,256,128]{3,2,1,0:T(8,128)(2,1)} %get-tuple-element.8, bf16[6,8,256,128]{3,2,1,0:T(8,128)(2,1)} %copy-done.6, bf16[6,8,256,128]{3,2,1,0:T(8,128)(2,1)S(1)} %copy-done.3, bf16[6,8,256,128]{3,2,1,0:T(8,128)(2,1)S(1)} %copy-done.1), kind=kOutput, calls=%fused_computation.40 | convolution fusion | flops 38711328768 | bytes 17825792 | tf_op jit(solution)/shard_map/dot_general | solution.py:29
  294.9 0.0 all-reduce.5.cloned.1.call-update
  294.9 94.7 %all-reduce.5.cloned.1.call-done = f32[512,512]{1,0:T(8,128)} async-done(((f32[512,512]{1,0:T(8,128)}), f32[512,512]{1,0:T(8,128)}) %all-reduce.5.cloned.1.call-update) | async-done | bytes 1048592 | tf_op jit(solution)/shard_map/psum | solution.py:79
  389.6 1.6 multiply_bitcast_fusion
  (12 shorter events, 0.0 us)
Async XLA Ops:
  6.5 26.9 %copy-start.4 = (bf16[6,8,256,128]{3,2,1,0:T(8,128)(2,1)S(1)}, bf16[6,8,256,128]{3,2,1,0:T(8,128)(2,1)}, u32[]{:S(2)}) copy-start(bf16[6,8,256,128]{3,2,1,0:T(8,128)(2,1)} %param.9) | copy-start | bytes 9437188
  6.5 8.9 %copy-start.7 = (f32[8,256]{1,0:T(8,128)S(1)}, f32[8,256]{1,0:T(8,128)}, u32[]{:S(2)}) copy-start(f32[8,256]{1,0:T(8,128)} %param.13) | copy-start | bytes 24580
  6.5 8.9 %copy-start.9 = (f32[128]{0:T(128)S(1)}, f32[128]{0:T(128)}, u32[]{:S(2)}) copy-start(f32[128]{0:T(128)} %param.14) | copy-start | bytes 1540
  6.5 238.2 %all-reduce.3.cloned.1.call-start = ((), (), s32[]{:S(2)}) async-start(), calls=%async_computation | async-start | bytes 4194304 | tf_op jit(solution)/shard_map/psum | solution.py:76
  6.5 26.9 %copy-start.5 = (bf16[6,8,256,128]{3,2,1,0:T(8,128)(2,1)S(1)}, bf16[6,8,256,128]{3,2,1,0:T(8,128)(2,1)}, u32[]{:S(2)}) copy-start(bf16[6,8,256,128]{3,2,1,0:T(8,128)(2,1)} %param.8) | copy-start | bytes 9437188
  8.8 22.9 %collective-permute-start = (bf16[2,6,2,256,128]{4,3,2,1,0:T(8,128)(2,1)S(1)}, bf16[2,6,2,256,128]{4,3,2,1,0:T(8,128)(2,1)S(1)}, u32[]{:S(2)}, u32[]{:S(2)}) collective-permute-start(bf16[2,6,2,256,128]{4,3,2,1,0:T(8,128)(2,1)S(1)} %get-tuple-element.19), channel_id=1, source_target_pairs={{0,1},{1,2},{2,3},{3,4},{4,5},{5,6},{6,7},{7,8},{8,9},{9,10},{10,1... | collective-permute-start | bytes 4718600 | tf_op jit(solution)/shard_map/ppermute | solution.py:12
  10.9 22.5 %collective-permute-start.1 = (bf16[2,6,2,256,128]{4,3,2,1,0:T(8,128)(2,1)S(1)}, bf16[2,6,2,256,128]{4,3,2,1,0:T(8,128)(2,1)S(1)}, u32[]{:S(2)}, u32[]{:S(2)}) collective-permute-start(bf16[2,6,2,256,128]{4,3,2,1,0:T(8,128)(2,1)S(1)} %get-tuple-element.20), channel_id=1, source_target_pairs={{1,0},{2,1},{3,2},{4,3},{5,4},{6,5},{7,6},{8,7},{9,8},{10,9},{11,1... | collective-permute-start | bytes 4718600 | tf_op jit(solution)/shard_map/ppermute | solution.py:15
  51.9 15.7 %copy-start.8 = (f32[8,256]{1,0:T(8,128)S(1)}, f32[8,256]{1,0:T(8,128)}, u32[]{:S(2)}) copy-start(f32[8,256]{1,0:T(8,128)} %param.12) | copy-start | bytes 24580
  67.6 27.2 %copy-start.10 = (f32[128]{0:T(128)S(1)}, f32[128]{0:T(128)}, u32[]{:S(2)}) copy-start(f32[128]{0:T(128)} %param.15) | copy-start | bytes 1540
  94.8 9.8 %copy-start = (bf16[6,8,256,128]{3,2,1,0:T(8,128)(2,1)}, bf16[6,8,256,128]{3,2,1,0:T(8,128)(2,1)S(1)}, u32[]{:S(2)}) copy-start(bf16[6,8,256,128]{3,2,1,0:T(8,128)(2,1)S(1)} %get-tuple-element.5) | copy-start | bytes 9437188
  94.8 11.5 %copy-start.2 = (bf16[6,8,256,128]{3,2,1,0:T(8,128)(2,1)S(1)}, bf16[6,8,256,128]{3,2,1,0:T(8,128)(2,1)}, u32[]{:S(2)}) copy-start(bf16[6,8,256,128]{3,2,1,0:T(8,128)(2,1)} %get-tuple-element.21) | copy-start | bytes 9437188
  104.6 1.7 copy-start.6
  114.4 132.7 %copy-start.1 = (bf16[6,8,256,128]{3,2,1,0:T(8,128)(2,1)S(1)}, bf16[6,8,256,128]{3,2,1,0:T(8,128)(2,1)}, u32[]{:S(2)}) copy-start(bf16[6,8,256,128]{3,2,1,0:T(8,128)(2,1)} %copy-done) | copy-start | bytes 9437188
  114.4 275.2 %all-reduce.5.cloned.1.call-start = ((), (), s32[]{:S(2)}) async-start(), calls=%async_computation.1 | async-start | bytes 2097152 | tf_op jit(solution)/shard_map/psum | solution.py:79
  244.7 2.5 copy-start.3
Sparse Core Ops, SparseCore 0:
  114.5 130.1 all-reduce.2
  295.0 94.4 all-reduce.4
where the time goes:
time: 398 us
  waiting for transfers between devices  241 us (61%)
  other arithmetic  69.8 us (18%)
  matrix products  47.7 us (12%)
  local copies, waits for them, and re-layouts  18.8 us (5%)
  between operations  13.5 us (3%)
  starting transfers between devices  6.82 us (2%)
    psum x1, waiting for transfers between devices, on_device(): lax.psum(local_sum.astype(jnp.bfloat16), 'member').astype(jnp.float32)  130 us
    psum x1, waiting for transfers between devices, on_device(): summed = lax.psum(gram_rows(anomaly, anomaly, highest), 'member')  94.7 us
    dot_general x1, matrix products, gram_rows(): lax.dot_general(left, right, (((0,), (0,)), ((), ())), preferred_element_...  47.7 us
    another operation x2, other arithmetic  37 us
    slice x2, local copies, waits for them, and re-layouts, lon_diff(): return (jnp.roll(field, -1, 2) - jnp.roll(field, 1, 2)) / 2.0  17 us
    ppermute x1, waiting for transfers between devices, extended(): lax.ppermute(lax.slice_in_dim(block, block.shape[dim] - width, None, axis...  14.9 us
    convert_element_type x1, other arithmetic, on_device(): v_full = padded[1].astype(jnp.float32)  12.8 us
    reduce_sum x1, other arithmetic, on_device(): local_sum = jnp.sum(sample_vector.astype(jnp.float32), axis=0)  8.08 us
  transfers between devices with their start and end apart: 4, of which 4 were waited for; matrix products, arithmetic and copies ran while one was open for 0% of the time, Pallas kernels for 0%

commit v1 on v0

--- a/solution.py
+++ b/solution.py
@@ -76,7 +76,7 @@
     totals = lax.psum(local_sum.astype(jnp.bfloat16), "member").astype(jnp.float32)
     ens_mean = totals / members_all
     anomaly = (sample_vector.astype(jnp.float32) - ens_mean[None]).reshape(-1, width)
-    summed = lax.psum(gram_rows(anomaly, anomaly, highest), "member")
+    summed = jnp.sum(lax.all_gather(gram_rows(anomaly, anomaly, highest), "member"), axis=0)
     mine = lax.dynamic_slice_in_dim(summed, lax.axis_index("member") * rows, rows, 0)
     return (mine * scale)[None]
 

time: 398 us -> 419 us (1.053)
  waiting for transfers between devices: 241 us -> 257 us
    all_gather x0 -> x1, waiting for transfers between devices: none -> 111 us  [on_device(): lax.all_gather(gram_rows(anomaly, anomaly, highest), 'member')]
    psum x1 -> x0, waiting for transfers between devices: 94.7 us -> none  [on_device(): summed = lax.psum(gram_rows(anomaly, anomaly, highest), 'member')]
    reduce_sum x0 -> x1, other arithmetic: none -> 4.49 us  [on_device(): jnp.sum(lax.all_gather(gram_rows(anomaly, anomaly, highest), 'member'), a...]
where the time goes in v1:
time: 419 us; the launch traced here: 418 us
  waiting for transfers between devices  257 us (61%)
  other arithmetic  73.4 us (18%)
  matrix products  47.7 us (11%)
  local copies, waits for them, and re-layouts  18.8 us (4%)
  between operations  13.5 us (3%)
  starting transfers between devices  6.82 us (2%)
    psum x1, waiting for transfers between devices, on_device(): lax.psum(local_sum.astype(jnp.bfloat16), 'member').astype(jnp.float32)  130 us
    all_gather x1, waiting for transfers between devices, on_device(): lax.all_gather(gram_rows(anomaly, anomaly, highest), 'member')  111 us
    dot_general x1, matrix products, gram_rows(): lax.dot_general(left, right, (((0,), (0,)), ((), ())), preferred_element_...  47.7 us
    another operation x2, other arithmetic  37 us
    slice x2, local copies, waits for them, and re-layouts, lon_diff(): return (jnp.roll(field, -1, 2) - jnp.roll(field, 1, 2)) / 2.0  17 us
    ppermute x1, waiting for transfers between devices, extended(): lax.ppermute(lax.slice_in_dim(block, block.shape[dim] - width, None, axis...  14.9 us
    convert_element_type x1, other arithmetic, on_device(): v_full = padded[1].astype(jnp.float32)  12.8 us
  transfers between devices with their start and end apart: 4, of which 4 were waited for; matrix products, arithmetic and copies ran while one was open for 0% of the time, Pallas kernels for 0%

profile of v1, /device:TPU:32, one launch (start us, length us, event | category | flops | bytes accessed | tf_op | source)
XLA Modules:
  0.0 417.7 jit_solution(14675721831401412600)
XLA Ops:
  6.5 0.0 all-reduce.2.cloned.1.call-start
  6.5 2.3 pad_maximum_fusion.4
  8.8 2.1 collective-permute-start
  10.9 4.5 %collective-permute-start.1 = (bf16[2,6,2,256,128]{4,3,2,1,0:T(8,128)(2,1)S(1)}, bf16[2,6,2,256,128]{4,3,2,1,0:T(8,128)(2,1)S(1)}, u32[]{:S(2)}, u32[]{:S(2)}) collective-permute-start(bf16[2,6,2,256,128]{4,3,2,1,0:T(8,128)(2,1)S(1)} %get-tuple-element.20), channel_id=1, source_target_pairs={{1,0},{2,1},{3,2},{4,3},{5,4},{6,5},{7,6},{8,7},{9,8},{10,9},{11,1... | collective-permute-start | bytes 4718600 | tf_op jit(solution)/shard_map/ppermute | solution.py:15
  15.4 0.0 copy-done.7
  15.4 0.0 copy-done.9
  15.5 1.3 broadcast_multiply_fusion
  16.8 14.9 %collective-permute-done = bf16[2,6,2,256,128]{4,3,2,1,0:T(8,128)(2,1)S(1)} collective-permute-done((bf16[2,6,2,256,128]{4,3,2,1,0:T(8,128)(2,1)S(1)}, bf16[2,6,2,256,128]{4,3,2,1,0:T(8,128)(2,1)S(1)}, u32[]{:S(2)}, u32[]{:S(2)}) %collective-permute-start) | collective-permute-done | bytes 1572896 | tf_op jit(solution)/shard_map/ppermute | solution.py:12
  31.7 1.7 collective-permute-done.1
  33.4 0.0 copy-done.4
  33.4 4.4 %pad_maximum_fusion.1 = bf16[2,6,12,256,128]{4,3,2,1,0:T(8,128)(2,1)} fusion(bf16[2,6,2,256,128]{4,3,2,1,0:T(8,128)(2,1)S(1)} %collective-permute-done.1, bf16[1,6,8,256,128]{4,3,2,1,0:T(8,128)(2,1)S(1)} %bitcast.22, bf16[1,6,8,256,128]{4,3,2,1,0:T(8,128)(2,1)S(1)} %bitcast.24, bf16[2,6,2,256,128]{4,3,2,1,0:T(8,128)(2,1)S(1)} %collective-permute-done), kind=kLoop, calls=%fused_computation.5 | loop fusion | flops 14155776 | bytes 18874368 | tf_op jit(solution)/shard_map/concatenate | solution.py:16
  37.8 12.8 %fusion.18 = (f32[6,12,256,128]{3,2,1,0:T(8,128)}, f32[6,12,256,128]{3,2,1,0:T(8,128)}) fusion(bf16[2,6,12,256,128]{4,3,2,1,0:T(8,128)(2,1)} %pad_maximum_fusion.1), kind=kLoop, calls=%fused_computation.34 | loop fusion | flops 4718592 | bytes 28311552 | tf_op jit(solution)/shard_map/convert_element_type | solution.py:51
  50.6 1.3 fusion.27
  51.9 0.0 copy-start.8
  51.9 15.6 %fusion.28 = (f32[6,8,255,128]{3,2,1,0:T(8,128)S(1)}, f32[6,8,255,128]{3,2,1,0:T(8,128)}, f32[6,8,255,128]{3,2,1,0:T(8,128)}, f32[6,8,255,128]{3,2,1,0:T(8,128)}) fusion(f32[6,12,256,128]{3,2,1,0:T(8,128)} %get-tuple-element.18, f32[6,12,256,128]{3,2,1,0:T(8,128)} %get-tuple-element.17), kind=kLoop, calls=%fused_computation.46 | loop fusion | bytes 50135040 | tf_op jit(solution)/shard_map/jit(_roll_static)/slice | solution.py:25
  67.6 0.0 copy-done.8
  67.6 27.2 %fusion.25 = (bf16[6,8,256,128]{3,2,1,0:T(8,128)(2,1)S(1)}, f32[6,8,256,128]{3,2,1,0:T(8,128)}, bf16[6,8,256,128]{3,2,1,0:T(8,128)(2,1)}) fusion(f32[6,12,256,128]{3,2,1,0:T(8,128)} %get-tuple-element.18, f32[6,8,255,128]{3,2,1,0:T(8,128)} %get-tuple-element.24, f32[6,8,1,128]{3,2,1,0:T(1,128)S(1)} %get-tuple-element.22, ...), kind=kLoop, calls=%fused_computation.44 | loop fusion | flops 44040192 | bytes 88088576 | tf_op jit(solution)/shard_map/convert.3
  94.8 9.8 %fusion.19 = (bf16[6,8,256,128]{3,2,1,0:T(8,128)(2,1)S(1)}, bf16[6,8,256,128]{3,2,1,0:T(8,128)(2,1)}) fusion(f32[6,8,256,128]{3,2,1,0:T(8,128)} %get-tuple-element.6, bf16[6,8,256,128]{3,2,1,0:T(8,128)(2,1)} %param.10, f32[8,256,128]{2,1,0:T(8,128)} %broadcast_multiply_fusion, f32[128]{0:T(128)S(1)} %copy-done.10, bf16[6,8,256,128]{3,2,1,0:T(8,128)(2,1)} %param.11), kind=kLoop, calls=%fused_computation.36 | loop fusion | flops 12582912 | bytes 19923456 | tf_op jit(solution)/shard_map/convert.5
  104.6 0.0 copy-done
  104.6 1.7 copy-done.6
  106.3 0.0 copy-done.2
  106.3 8.1 %fusion.20 = bf16[8,256,512]{2,1,0:T(8,128)(2,1)} fusion(bf16[6,8,256,128]{3,2,1,0:T(8,128)(2,1)} %get-tuple-element.8, bf16[6,8,256,128]{3,2,1,0:T(8,128)(2,1)S(1)} %get-tuple-element.7, bf16[6,8,256,128]{3,2,1,0:T(8,128)(2,1)S(1)} %copy-done.2, bf16[6,8,256,128]{3,2,1,0:T(8,128)(2,1)S(1)} %get-tuple-element.5), kind=kLoop, calls=%fused_computation.37 | loop fusion | flops 55574528 | bytes 14680064 | tf_op jit(solution)/shard_map/reduce_sum | solution.py:74
  114.4 0.0 all-reduce.2.cloned.1.call-update
  114.4 0.2 all-gather.3.cloned.1.call-start
  114.6 130.1 %all-reduce.2.cloned.1.call-done = bf16[8,256,512]{2,1,0:T(8,128)(2,1)} async-done(((bf16[8,256,512]{2,1,0:T(8,128)(2,1)}), bf16[8,256,512]{2,1,0:T(8,128)(2,1)}) %all-reduce.2.cloned.1.call-update) | async-done | bytes 2097168 | tf_op jit(solution)/shard_map/psum | solution.py:76
  244.7 2.4 convert_multiply_fusion
  247.1 0.1 copy-done.3
  247.2 47.7 %fusion.21 = f32[512,512]{1,0:T(8,128)} fusion(f32[8,256,512]{2,1,0:T(8,128)S(1)} %convert_multiply_fusion, bf16[6,8,256,128]{3,2,1,0:T(8,128)(2,1)} %get-tuple-element.8, bf16[6,8,256,128]{3,2,1,0:T(8,128)(2,1)} %copy-done.6, bf16[6,8,256,128]{3,2,1,0:T(8,128)(2,1)S(1)} %copy-done.3, bf16[6,8,256,128]{3,2,1,0:T(8,128)(2,1)S(1)} %copy-done.1), kind=kOutput, calls=%fused_computation.40 | convolution fusion | flops 38711328768 | bytes 17825792 | tf_op jit(solution)/shard_map/dot_general | solution.py:29
  295.0 0.0 all-gather.3.cloned.1.call-update
  295.0 110.7 %all-gather.3.cloned.1.call-done = f32[4096,512]{1,0:T(8,128)} async-done(((f32[512,512]{1,0:T(8,128)}), f32[4096,512]{1,0:T(8,128)}) %all-gather.3.cloned.1.call-update) | async-done | bytes 8388624 | tf_op jit(solution)/shard_map/all_gather | solution.py:79
  405.7 4.5 %reduce_sum.22 = f32[512,512]{1,0:T(8,128)S(1)} reduce(f32[8,512,512]{2,1,0:T(8,128)} %bitcast.25, f32[]{:T(128)} %constant.24.clone.1), dimensions={0}, to_apply=%region_2.3 | reduce | flops 1835008 | bytes 9437188 | tf_op jit(solution)/shard_map/reduce_sum | solution.py:79
  410.2 0.7 multiply_bitcast_fusion
  (13 shorter events, 0.0 us)
Async XLA Ops:
  6.5 26.9 %copy-start.4 = (bf16[6,8,256,128]{3,2,1,0:T(8,128)(2,1)S(1)}, bf16[6,8,256,128]{3,2,1,0:T(8,128)(2,1)}, u32[]{:S(2)}) copy-start(bf16[6,8,256,128]{3,2,1,0:T(8,128)(2,1)} %param.9) | copy-start | bytes 9437188
  6.5 8.9 %copy-start.7 = (f32[8,256]{1,0:T(8,128)S(1)}, f32[8,256]{1,0:T(8,128)}, u32[]{:S(2)}) copy-start(f32[8,256]{1,0:T(8,128)} %param.13) | copy-start | bytes 24580
  6.5 8.9 %copy-start.9 = (f32[128]{0:T(128)S(1)}, f32[128]{0:T(128)}, u32[]{:S(2)}) copy-start(f32[128]{0:T(128)} %param.14) | copy-start | bytes 1540
  6.5 238.2 %all-reduce.2.cloned.1.call-start = ((), (), s32[]{:S(2)}) async-start(), calls=%async_computation | async-start | bytes 4194304 | tf_op jit(solution)/shard_map/psum | solution.py:76
  6.5 26.9 %copy-start.5 = (bf16[6,8,256,128]{3,2,1,0:T(8,128)(2,1)S(1)}, bf16[6,8,256,128]{3,2,1,0:T(8,128)(2,1)}, u32[]{:S(2)}) copy-start(bf16[6,8,256,128]{3,2,1,0:T(8,128)(2,1)} %param.8) | copy-start | bytes 9437188
  8.8 22.9 %collective-permute-start = (bf16[2,6,2,256,128]{4,3,2,1,0:T(8,128)(2,1)S(1)}, bf16[2,6,2,256,128]{4,3,2,1,0:T(8,128)(2,1)S(1)}, u32[]{:S(2)}, u32[]{:S(2)}) collective-permute-start(bf16[2,6,2,256,128]{4,3,2,1,0:T(8,128)(2,1)S(1)} %get-tuple-element.19), channel_id=1, source_target_pairs={{0,1},{1,2},{2,3},{3,4},{4,5},{5,6},{6,7},{7,8},{8,9},{9,10},{10,1... | collective-permute-start | bytes 4718600 | tf_op jit(solution)/shard_map/ppermute | solution.py:12
  10.9 22.5 %collective-permute-start.1 = (bf16[2,6,2,256,128]{4,3,2,1,0:T(8,128)(2,1)S(1)}, bf16[2,6,2,256,128]{4,3,2,1,0:T(8,128)(2,1)S(1)}, u32[]{:S(2)}, u32[]{:S(2)}) collective-permute-start(bf16[2,6,2,256,128]{4,3,2,1,0:T(8,128)(2,1)S(1)} %get-tuple-element.20), channel_id=1, source_target_pairs={{1,0},{2,1},{3,2},{4,3},{5,4},{6,5},{7,6},{8,7},{9,8},{10,9},{11,1... | collective-permute-start | bytes 4718600 | tf_op jit(solution)/shard_map/ppermute | solution.py:15
  51.9 15.7 %copy-start.8 = (f32[8,256]{1,0:T(8,128)S(1)}, f32[8,256]{1,0:T(8,128)}, u32[]{:S(2)}) copy-start(f32[8,256]{1,0:T(8,128)} %param.12) | copy-start | bytes 24580
  67.6 27.2 %copy-start.10 = (f32[128]{0:T(128)S(1)}, f32[128]{0:T(128)}, u32[]{:S(2)}) copy-start(f32[128]{0:T(128)} %param.15) | copy-start | bytes 1540
  94.8 9.8 %copy-start = (bf16[6,8,256,128]{3,2,1,0:T(8,128)(2,1)}, bf16[6,8,256,128]{3,2,1,0:T(8,128)(2,1)S(1)}, u32[]{:S(2)}) copy-start(bf16[6,8,256,128]{3,2,1,0:T(8,128)(2,1)S(1)} %get-tuple-element.5) | copy-start | bytes 9437188
  94.8 11.5 %copy-start.2 = (bf16[6,8,256,128]{3,2,1,0:T(8,128)(2,1)S(1)}, bf16[6,8,256,128]{3,2,1,0:T(8,128)(2,1)}, u32[]{:S(2)}) copy-start(bf16[6,8,256,128]{3,2,1,0:T(8,128)(2,1)} %get-tuple-element.21) | copy-start | bytes 9437188
  104.6 1.7 copy-start.6
  114.4 132.7 %copy-start.1 = (bf16[6,8,256,128]{3,2,1,0:T(8,128)(2,1)S(1)}, bf16[6,8,256,128]{3,2,1,0:T(8,128)(2,1)}, u32[]{:S(2)}) copy-start(bf16[6,8,256,128]{3,2,1,0:T(8,128)(2,1)} %copy-done) | copy-start | bytes 9437188
  114.4 291.3 %all-gather.3.cloned.1.call-start = ((), (), s32[]{:S(2)}) async-start(), calls=%async_computation.1 | async-start | bytes 9437184 | tf_op jit(solution)/shard_map/all_gather | solution.py:79
  244.7 2.5 copy-start.3
Sparse Core Ops, SparseCore 0:
  114.5 130.1 all-reduce.1
  295.1 110.5 all-gather.2
